TPU v7x, 32 devices: a whole 2x2x4 slice. The times are simulated.
32 devices in a mesh: dp: 8 (over y, x, core), tensor: 4 (over z).
Axes of the slice: x: 2, y: 2, z: 4, core: 2. Of those that a mesh axis runs over, the one named last changes fastest.
Arguments:
- block_input: bfloat16 [8192, 1024], P(('dp', 'tensor')), may hold values from -24 to 24
- lengths: int32 [8], P('dp'), may hold values from 128 to 1024, as said below
- query_weight: bfloat16 [1024, 1024], P('dp', 'tensor'), may hold values from -0.1875 to 0.1875
- key_weight: bfloat16 [1024, 1024], P('dp', 'tensor'), may hold values from -0.1875 to 0.1875
- value_weight: bfloat16 [1024, 1024], P('dp', 'tensor'), may hold values from -0.1875 to 0.1875
- query_bias: bfloat16 [1024], P(('tensor', 'dp')), may hold values from -4 to 4
- value_bias: bfloat16 [1024], P(('tensor', 'dp')), may hold values from -4 to 4
- output_weight: bfloat16 [1024, 1024], P('tensor', 'dp'), may hold values from -0.75 to 0.75
- output_bias: float32 [1024], P(('dp', 'tensor')), may hold values from -4 to 4
- first_gain: float32 [1024], P(('dp', 'tensor')), may hold values from 0.1 to 1.9
- first_shift: float32 [1024], P(('dp', 'tensor')), may hold values from -3 to 3
- inner_weight: bfloat16 [1024, 4096], P('dp', 'tensor'), may hold values from -0.1875 to 0.1875
- inner_bias: bfloat16 [4096], P(('tensor', 'dp')), may hold values from -3 to 3
- outer_weight: bfloat16 [4096, 1024], P('tensor', 'dp'), may hold values from -0.09375 to 0.09375
- outer_bias: float32 [1024], P(('dp', 'tensor')), may hold values from -4 to 4
- second_gain: float32 [1024], P(('dp', 'tensor')), may hold values from 0.1 to 1.9
- second_shift: float32 [1024], P(('dp', 'tensor')), may hold values from -3 to 3
- cotangent: bfloat16 [8192, 1024], P(('dp', 'tensor')), may hold values from -6 to 6
Outputs:
- block_output: bfloat16 [8192, 1024], P(('dp', 'tensor'))
- input_grad: float32 [8192, 1024], P(('dp', 'tensor'))
- query_weight_grad: float32 [1024, 1024], P('dp', 'tensor')
- key_weight_grad: float32 [1024, 1024], P('dp', 'tensor')
- value_weight_grad: float32 [1024, 1024], P('dp', 'tensor')
- query_bias_grad: float32 [1024], P(('tensor', 'dp'))
- value_bias_grad: float32 [1024], P(('tensor', 'dp'))
- output_weight_grad: float32 [1024, 1024], P('tensor', 'dp')
- output_bias_grad: float32 [1024], P(('dp', 'tensor'))
- first_gain_grad: float32 [1024], P(('dp', 'tensor'))
- first_shift_grad: float32 [1024], P(('dp', 'tensor'))
- inner_weight_grad: float32 [1024, 4096], P('dp', 'tensor')
- inner_bias_grad: float32 [4096], P(('tensor', 'dp'))
- outer_weight_grad: float32 [4096, 1024], P('tensor', 'dp')
- outer_bias_grad: float32 [1024], P(('dp', 'tensor'))
- second_gain_grad: float32 [1024], P(('dp', 'tensor'))
- second_shift_grad: float32 [1024], P(('dp', 'tensor'))
Inputs may be any that keep to these rules, and one draw needn't show every extreme that they name: lengths[s] tokens at the start of sequence s are valid keys; one sequence is full and one has the fewest.
All inputs are finite; a program needn't handle non-finite values.
Results may differ from a plain program's by a relative error of at most 0.009.
The roundings to bfloat16 on the way count: a program that leaves them out, or rounds other values in their place, can miss the bound.
Values may be sent and summed in bfloat16 or wider, within the bound.
A program may use at most 128 MiB of HBM per device.

v0:
```python
import jax
import jax.numpy as jnp
from jax import lax
from jax.sharding import PartitionSpec as P

HEAD_DIM = 64


inv_root2 = 0.7071067811865476
inv_root2pi = 0.3989422804014327
norm_eps = 1e-06


def gelu_cdf(values):
    return 0.5 * (1.0 + jax.scipy.special.erf(values * inv_root2))


def row_norm(resid_rows, norm_gain, norm_shift):
    center = resid_rows - jnp.mean(resid_rows, axis=-1, keepdims=True)
    inverse = lax.rsqrt(jnp.mean(center * center, axis=-1, keepdims=True) + norm_eps)
    return center * inverse * norm_gain + norm_shift


def norm_back(resid_rows, norm_gain, upstream):
    center = resid_rows - jnp.mean(resid_rows, axis=-1, keepdims=True)
    inverse = lax.rsqrt(jnp.mean(center * center, axis=-1, keepdims=True) + norm_eps)
    normed = center * inverse
    scaled_up = upstream * norm_gain
    d_resid = inverse * (
        scaled_up
        - jnp.mean(scaled_up, axis=-1, keepdims=True)
        - normed * jnp.mean(scaled_up * normed, axis=-1, keepdims=True)
    )
    return (d_resid, jnp.sum(upstream * normed, axis=0), jnp.sum(upstream, axis=0))


def dense(left, right):
    return jnp.dot(left, right, preferred_element_type=jnp.float32)


def dense_tn(left, right):
    return lax.dot_general(
        left, right, (((0,), (0,)), ((), ())), preferred_element_type=jnp.float32
    )


def dense_nt(left, right):
    return lax.dot_general(
        left, right, (((1,), (1,)), ((), ())), preferred_element_type=jnp.float32
    )


def whole_rows(part_rows):
    return lax.all_gather(part_rows, "tensor", axis=0, tiled=True)


def share_rows(partial_value):
    return lax.psum_scatter(partial_value, "tensor", scatter_dimension=0, tiled=True)


def whole_grads(part_rows):
    return lax.all_gather(part_rows, "tensor", axis=0, tiled=True)


def share_grads(partial_value):
    return lax.psum_scatter(partial_value, "tensor", scatter_dimension=0, tiled=True)


def masked_scores(q_block, k_seq, key_valid):
    scores = jnp.einsum(
        "qhd,khd->hqk", q_block, k_seq, preferred_element_type=jnp.float32
    ) * HEAD_DIM ** (-0.5)
    return jnp.where(key_valid[None, None, :], scores, -jnp.inf)


def attention_fwd(q_rows, k_rows, v_rows, lengths):
    seq_count = lengths.shape[0]
    seq_len = q_rows.shape[0] // seq_count
    heads_here = q_rows.shape[1] // HEAD_DIM
    block_rows = min(512, seq_len)
    block_count = seq_len // block_rows
    head_shape = (seq_count, seq_len, heads_here, HEAD_DIM)

    def one_sequence(pieces):
        q_seq, k_seq, v_seq, length = pieces
        key_valid = jnp.arange(seq_len) < length

        def one_block(q_block):
            scores = masked_scores(q_block, k_seq, key_valid)
            row_top = jnp.max(scores, axis=-1, keepdims=True)
            log_total = row_top + jnp.log(
                jnp.sum(jnp.exp(scores - row_top), axis=-1, keepdims=True)
            )
            probs_b = jnp.exp(scores - log_total).astype(jnp.bfloat16)
            context = jnp.einsum("hqk,khd->qhd", probs_b, v_seq, preferred_element_type=jnp.float32)
            return (context.astype(jnp.bfloat16), log_total[..., 0])

        return lax.map(one_block, q_seq.reshape(block_count, block_rows, heads_here, HEAD_DIM))

    context, log_total = lax.map(
        one_sequence,
        (
            q_rows.reshape(head_shape),
            k_rows.reshape(head_shape),
            v_rows.reshape(head_shape),
            lengths,
        ),
    )
    return (context.reshape(q_rows.shape), log_total)


def attention_bwd(q_rows, k_rows, v_rows, lengths, log_total, d_context):
    seq_count = lengths.shape[0]
    seq_len = q_rows.shape[0] // seq_count
    heads_here = q_rows.shape[1] // HEAD_DIM
    block_rows = min(512, seq_len)
    block_count = seq_len // block_rows
    head_shape = (seq_count, seq_len, heads_here, HEAD_DIM)
    block_shape = (block_count, block_rows, heads_here, HEAD_DIM)

    def one_sequence(pieces):
        q_seq, k_seq, v_seq, length, lse_seq, dctx_seq = pieces
        key_valid = jnp.arange(seq_len) < length

        def one_block(running, block_pieces):
            q_block, lse_block, dctx_block = block_pieces
            scores = masked_scores(q_block, k_seq, key_valid)
            attn_probs = jnp.exp(scores - lse_block[..., None])
            probs_b = attn_probs.astype(jnp.bfloat16)
            d_probs = jnp.einsum(
                "qhd,khd->hqk", dctx_block, v_seq, preferred_element_type=jnp.float32
            )
            row_inner = jnp.sum(attn_probs * d_probs, axis=-1, keepdims=True)
            d_scores = (attn_probs * (d_probs - row_inner) * HEAD_DIM ** (-0.5)).astype(
                jnp.bfloat16
            )
            d_query = jnp.einsum(
                "hqk,khd->qhd", d_scores, k_seq, preferred_element_type=jnp.float32
            )
            key_sum = running[0] + jnp.einsum(
                "hqk,qhd->khd", d_scores, q_block, preferred_element_type=jnp.float32
            )
            value_sum = running[1] + jnp.einsum(
                "hqk,qhd->khd", probs_b, dctx_block, preferred_element_type=jnp.float32
            )
            return ((key_sum, value_sum), d_query)

        zero_grad = jnp.zeros(k_seq.shape, jnp.float32)
        block_inputs = (q_seq.reshape(block_shape), lse_seq, dctx_seq.reshape(block_shape))
        (key_sum, value_sum), d_query = lax.scan(one_block, (zero_grad, zero_grad), block_inputs)
        return (d_query, key_sum, value_sum)

    d_query, d_key, d_value = lax.map(
        one_sequence,
        (
            q_rows.reshape(head_shape),
            k_rows.reshape(head_shape),
            v_rows.reshape(head_shape),
            lengths,
            log_total,
            d_context.reshape(head_shape),
        ),
    )
    return (
        d_query.reshape(q_rows.shape),
        d_key.reshape(q_rows.shape),
        d_value.reshape(q_rows.shape),
    )


def per_device(
    block_input,
    lengths,
    query_weight,
    key_weight,
    value_weight,
    query_bias,
    value_bias,
    output_weight,
    output_bias,
    first_gain,
    first_shift,
    inner_weight,
    inner_bias,
    outer_weight,
    outer_bias,
    second_gain,
    second_shift,
    cotangent,
):
    fetched = (
        lax.all_gather(query_weight, "dp", axis=0, tiled=True),
        lax.all_gather(key_weight, "dp", axis=0, tiled=True),
        lax.all_gather(value_weight, "dp", axis=0, tiled=True),
        lax.all_gather(output_weight, "dp", axis=1, tiled=True),
        lax.all_gather(inner_weight, "dp", axis=0, tiled=True),
        lax.all_gather(outer_weight, "dp", axis=1, tiled=True),
        lax.all_gather(query_bias, "dp", axis=0, tiled=True),
        lax.all_gather(value_bias, "dp", axis=0, tiled=True),
        lax.all_gather(inner_bias, "dp", axis=0, tiled=True),
    )
    (
        wide_query,
        wide_key,
        wide_value,
        wide_output,
        wide_inner,
        wide_outer,
        bias_query,
        bias_value,
        bias_inner,
    ) = fetched
    vectors = (
        lax.all_gather(output_bias, ("dp", "tensor"), axis=0, tiled=True),
        lax.all_gather(first_gain, ("dp", "tensor"), axis=0, tiled=True),
        lax.all_gather(first_shift, ("dp", "tensor"), axis=0, tiled=True),
        lax.all_gather(outer_bias, ("dp", "tensor"), axis=0, tiled=True),
        lax.all_gather(second_gain, ("dp", "tensor"), axis=0, tiled=True),
        lax.all_gather(second_shift, ("dp", "tensor"), axis=0, tiled=True),
    )
    full_obias, full_gain1, full_shift1, full_bias2, full_gain2, full_shift2 = vectors
    seq_rows = whole_rows(block_input)
    q_rows = (dense(seq_rows, wide_query) + bias_query.astype(jnp.float32)).astype(jnp.bfloat16)
    k_rows = dense(seq_rows, wide_key).astype(jnp.bfloat16)
    v_rows = (dense(seq_rows, wide_value) + bias_value.astype(jnp.float32)).astype(jnp.bfloat16)
    context, log_total = attention_fwd(q_rows, k_rows, v_rows, lengths)
    own_context = lax.all_to_all(context, "tensor", split_axis=0, concat_axis=1, tiled=True)
    all_output = lax.all_gather(wide_output, "tensor", axis=0, tiled=True)
    attn_sum = dense(own_context, all_output)
    resid_one = block_input.astype(jnp.float32) + attn_sum + full_obias
    middle = row_norm(resid_one, full_gain1, full_shift1)
    middle_rows = whole_rows(middle.astype(jnp.bfloat16))
    pre_act = dense(middle_rows, wide_inner) + bias_inner.astype(jnp.float32)
    hidden_b = (pre_act * gelu_cdf(pre_act)).astype(jnp.bfloat16)
    resid_two = middle + share_rows(dense(hidden_b, wide_outer)) + full_bias2
    block_output = row_norm(resid_two, full_gain2, full_shift2).astype(jnp.bfloat16)
    regathered = (
        lax.all_gather(query_weight, "dp", axis=0, tiled=True),
        lax.all_gather(key_weight, "dp", axis=0, tiled=True),
        lax.all_gather(value_weight, "dp", axis=0, tiled=True),
        lax.all_gather(output_weight, "dp", axis=1, tiled=True),
        lax.all_gather(inner_weight, "dp", axis=0, tiled=True),
        lax.all_gather(outer_weight, "dp", axis=1, tiled=True),
    )
    back_query, back_key, back_value, back_output, back_inner, back_outer = regathered
    d_resid2, gain2_grad, shift2_grad = norm_back(
        resid_two, full_gain2, cotangent.astype(jnp.float32)
    )
    ffn_rows = whole_grads(d_resid2.astype(jnp.bfloat16))
    outer_grad = dense_tn(hidden_b, ffn_rows)
    gelu_slope = gelu_cdf(pre_act) + pre_act * inv_root2pi * jnp.exp(-0.5 * pre_act * pre_act)
    d_pre = dense_nt(ffn_rows, back_outer) * gelu_slope
    d_pre_b = d_pre.astype(jnp.bfloat16)
    inner_grad = dense_tn(middle_rows, d_pre_b)
    ibias_grad = jnp.sum(d_pre, axis=0)
    d_middle = share_grads(dense_nt(d_pre_b, back_inner)) + d_resid2
    d_resid1, gain1_grad, shift1_grad = norm_back(resid_one, full_gain1, d_middle)
    attn_rows = whole_grads(d_resid1.astype(jnp.bfloat16))
    output_grad = dense_tn(context, attn_rows)
    d_context = dense_nt(attn_rows, back_output).astype(jnp.bfloat16)
    d_query, d_key, d_value = attention_bwd(q_rows, k_rows, v_rows, lengths, log_total, d_context)
    dq_b = d_query.astype(jnp.bfloat16)
    dk_b = d_key.astype(jnp.bfloat16)
    dv_b = d_value.astype(jnp.bfloat16)
    query_grad = dense_tn(seq_rows, dq_b)
    key_grad = dense_tn(seq_rows, dk_b)
    value_grad = dense_tn(seq_rows, dv_b)
    qbias_grad = jnp.sum(d_query, axis=0)
    vbias_grad = jnp.sum(d_value, axis=0)
    input_grad = (
        share_grads(
            dense_nt(dq_b, back_query) + dense_nt(dk_b, back_key) + dense_nt(dv_b, back_value)
        )
        + d_resid1
    )
    all_sent = (
        lax.psum_scatter(query_grad, "dp", scatter_dimension=0, tiled=True),
        lax.psum_scatter(key_grad, "dp", scatter_dimension=0, tiled=True),
        lax.psum_scatter(value_grad, "dp", scatter_dimension=0, tiled=True),
        lax.psum_scatter(output_grad, "dp", scatter_dimension=1, tiled=True),
        lax.psum_scatter(inner_grad, "dp", scatter_dimension=0, tiled=True),
        lax.psum_scatter(outer_grad, "dp", scatter_dimension=1, tiled=True),
        lax.psum_scatter(qbias_grad, "dp", scatter_dimension=0, tiled=True),
        lax.psum_scatter(vbias_grad, "dp", scatter_dimension=0, tiled=True),
        lax.psum_scatter(ibias_grad, "dp", scatter_dimension=0, tiled=True),
    )
    sent_query, sent_key, sent_value, sent_output, sent_inner, sent_outer = all_sent[:6]
    sent_qbias, sent_vbias, sent_ibias = all_sent[6:]
    vector_sent = (
        lax.psum_scatter(
            jnp.sum(d_resid1, axis=0), ("dp", "tensor"), scatter_dimension=0, tiled=True
        ),
        lax.psum_scatter(gain1_grad, ("dp", "tensor"), scatter_dimension=0, tiled=True),
        lax.psum_scatter(shift1_grad, ("dp", "tensor"), scatter_dimension=0, tiled=True),
        lax.psum_scatter(
            jnp.sum(d_resid2, axis=0), ("dp", "tensor"), scatter_dimension=0, tiled=True
        ),
        lax.psum_scatter(gain2_grad, ("dp", "tensor"), scatter_dimension=0, tiled=True),
        lax.psum_scatter(shift2_grad, ("dp", "tensor"), scatter_dimension=0, tiled=True),
    )
    sent_obias, sent_gain1, sent_shift1, sent_bias2, sent_gain2, sent_shift2 = vector_sent
    return (
        block_output,
        input_grad,
        sent_query,
        sent_key,
        sent_value,
        sent_qbias,
        sent_vbias,
        sent_output,
        sent_obias,
        sent_gain1,
        sent_shift1,
        sent_inner,
        sent_ibias,
        sent_outer,
        sent_bias2,
        sent_gain2,
        sent_shift2,
    )


def solution(mesh):
    return jax.shard_map(
        per_device,
        mesh=mesh,
        in_specs=(
            P(("dp", "tensor"), None),
            P("dp"),
            P("dp", "tensor"),
            P("dp", "tensor"),
            P("dp", "tensor"),
            P(("tensor", "dp")),
            P(("tensor", "dp")),
            P("tensor", "dp"),
            P(("dp", "tensor")),
            P(("dp", "tensor")),
            P(("dp", "tensor")),
            P("dp", "tensor"),
            P(("tensor", "dp")),
            P("tensor", "dp"),
            P(("dp", "tensor")),
            P(("dp", "tensor")),
            P(("dp", "tensor")),
            P(("dp", "tensor"), None),
        ),
        out_specs=(
            P(("dp", "tensor"), None),
            P(("dp", "tensor"), None),
            P("dp", "tensor"),
            P("dp", "tensor"),
            P("dp", "tensor"),
            P(("tensor", "dp")),
            P(("tensor", "dp")),
            P("tensor", "dp"),
            P(("dp", "tensor")),
            P(("dp", "tensor")),
            P(("dp", "tensor")),
            P("dp", "tensor"),
            P(("tensor", "dp")),
            P("tensor", "dp"),
            P(("dp", "tensor")),
            P(("dp", "tensor")),
            P(("dp", "tensor")),
        ),
        check_vma=False,
    )
```

profile of v0, /device:TPU:0, one launch (start us, length us, event | category | flops | bytes accessed | tf_op | source)
XLA Modules:
  0.0 965.9 jit_solution(14071781136439694650)
XLA Ops:
  8.0 13.4 %all_gather.72 = bf16[256,1024]{1,0:T(8,128)(2,1)} all-gather(bf16[256,128]{1,0:T(8,128)(2,1)} %param.29), channel_id=1, replica_groups=mesh['dp'=8,'tensor'=4] {'dp'}, dimensions={1}, use_global_device_ids=true | all-gather | bytes 589824 | tf_op jit(solution)/shard_map/all_gather | solution.py:195
  25.8 14.0 %all-reduce.20 = (bf16[256]{0:T(256)(128)(2,1)S(1)}, bf16[256]{0:T(256)(128)(2,1)S(1)}) all-reduce(bf16[256]{0:T(256)(128)(2,1)S(1)} %dynamic-update-slice, bf16[256]{0:T(256)(128)(2,1)S(1)} %dynamic-update-slice.1), channel_id=1, replica_groups=mesh['dp'=8,'tensor'=4] {'dp'}, use_global_device_ids=true, to_apply=%add | all-reduce | flops 512 | bytes 2048
  39.9 9.2 all_gather.67
  49.0 9.5 all_gather.69
  58.6 9.2 all_gather.70
  67.7 2.5 fusion.98
  71.3 2.4 convolution_convert_fusion.1
  73.7 2.4 fusion.99
  76.0 14.0 %while.48 = (s32[]{:T(128)}, bf16[2,512,4,64]{1,3,2,0:T(8,128)(2,1)}, f32[2,4,512]{2,1,0:T(4,128)S(1)}, bf16[2,512,4,64]{1,3,2,0:T(8,128)(2,1)S(1)}, bf16[1024,4...) while((s32[]{:T(128)}, ...), condition=%wide.region_3.4_spmd.clone, body=%wide.region_0.3_spmd.clone.sunk | while | flops 560069632 | bytes 31002788 | solution.py:98
  78.1 2.0 exponential_reduce_fusion.2
  80.1 2.1 fusion.187
  85.1 2.0 exponential_reduce_fusion.2
  87.1 2.1 fusion.187
  90.0 1.8 copy.55
  92.9 5.0 all-to-all-start
  99.1 40.6 %all-reduce.18 = (f32[1024]{0:T(1024)S(1)}, f32[1024]{0:T(1024)S(1)}, f32[1024]{0:T(1024)S(1)}, f32[1024]{0:T(1024)S(1)}, f32[1024]{0:T(1024)S(1)}) all-reduce(f32[1024]{0:T(1024)S(1)} %dynamic-update-slice.2, f32[1024]{0:T(1024)S(1)} %dynamic-update-slice.4, ...), channel_id=1, replica_groups=mesh['dp'=8,'tensor'=4] {'dp','tensor'}, use_global_device_ids=true, to_apply=%add.2 | all-reduce | flops 5120 | bytes 40960
  140.5 2.6 fusion.117
  145.2 9.6 all-gather
  154.8 36.0 %all-gather.13.cloned.1.call-done = bf16[1024,1024]{1,0:T(8,128)(2,1)} async-done(((bf16[256,1024]{1,0:T(8,128)(2,1)}), bf16[1024,1024]{1,0:T(8,128)(2,1)}) %all-gather.13.cloned.1.call-update) | async-done | bytes 2097168 | tf_op jit(solution)/shard_map/all_gather | solution.py:54
  190.8 7.5 multiply_convert_fusion.1
  198.2 21.2 %all-gather.17.cloned.1.call-done = bf16[1024,1024]{1,0:T(8,128)(2,1)} async-done(((bf16[1024,128]{1,0:T(8,128)(2,1)}), bf16[1024,1024]{1,0:T(8,128)(2,1)}) %all-gather.17.cloned.1.call-update) | async-done | bytes 2097168 | tf_op jit(solution)/shard_map/all_gather | solution.py:197
  219.4 6.5 fusion.119
  226.0 76.9 %reduce-scatter.10.cloned.1.call-done = f32[256,1024]{1,0:T(8,128)} async-done(((f32[1024,1024]{1,0:T(8,128)}), f32[256,1024]{1,0:T(8,128)}) %reduce-scatter.10.cloned.1.call-update) | async-done | bytes 1048592 | tf_op jit(solution)/shard_map/reduce_scatter | solution.py:58
  302.9 1.6 fusion.112
  304.8 1.6 fusion.103
  309.8 46.3 %all-gather.19.cloned.1.call-done = bf16[1024,1024]{1,0:T(8,128)(2,1)} async-done(((bf16[256,1024]{1,0:T(8,128)(2,1)}), bf16[1024,1024]{1,0:T(8,128)(2,1)}) %all-gather.19.cloned.1.call-update) | async-done | bytes 2097168 | tf_op jit(solution)/shard_map/all_gather | solution.py:62
  356.0 6.6 fusion.118
  364.0 4.3 fusion.106
  368.6 75.5 %reduce-scatter.12.cloned.1.call-done = f32[256,1024]{1,0:T(8,128)} async-done(((f32[1024,1024]{1,0:T(8,128)}), f32[256,1024]{1,0:T(8,128)}) %reduce-scatter.12.cloned.1.call-update) | async-done | bytes 1048592 | tf_op jit(solution)/shard_map/reduce_scatter | solution.py:66
  444.1 2.1 multiply_reduce_fusion.1
  447.8 46.2 %all-gather.21.cloned.1.call-done = bf16[1024,1024]{1,0:T(8,128)(2,1)} async-done(((bf16[256,1024]{1,0:T(8,128)(2,1)}), bf16[1024,1024]{1,0:T(8,128)(2,1)}) %all-gather.21.cloned.1.call-update) | async-done | bytes 2097168 | tf_op jit(solution)/shard_map/all_gather | solution.py:62
  494.0 2.4 convolution_convert_fusion
  497.8 1.6 copy.59
  499.4 110.3 %while.49 = (s32[]{:T(128)}, f32[1024,4,64]{0,2,1:T(8,128)}, f32[1024,4,64]{0,2,1:T(8,128)}, f32[2,512,4,64]{1,3,2,0:T(8,128)}, bf16[2,512,4,64]{1,3,2,0:T(8,128...) while((s32[]{:T(128)}, f32[1024,4,64]{0,2,1:T(8,128)}, ...), condition=%wide.region_16.17_spmd.clone, body=%wide.region_14.16_spmd.clone.sunk | while | flops 1397758976 | bytes 133232840 | solution.py:150
  501.4 3.5 fusion.201
  504.9 4.5 fusion.198
  509.4 22.7 %fusion.200 = f32[1024,4,64]{0,2,1:T(8,128)} fusion(f32[4,512,1024]{2,1,0:T(8,128)} %fusion.198, f32[4,512,1024]{2,1,0:T(8,128)} %copy-done, f32[4,512]{1,0:T(4,128)S(1)} %dynamic-slice_bitcast_fusion.2, pred[1024]{0:T(1024)(128)(4,1)S(1)} %iota_compare_fusion.5, f32[1024,4,64]{0,2,1:T(8,128)} %get-tuple-element.557, pred[]{:T(512)S(6)} %compare.3, ...), kind=kOutput, calls=%fused_computation.40.clone.1 | convolution fusion | flops 292031488 | bytes 35932164 | tf_op jit(solution)/shard_map/while/body/eval_jaxpr/while/body/eval_jaxpr/hqk,qhd->khd/dot_general | solution.py:140
  532.1 22.1 %fusion.202 = f32[2,512,4,64]{1,3,2,0:T(8,128)} fusion(f32[2,512,4,64]{1,3,2,0:T(8,128)} %get-tuple-element.559, s32[]{:T(128)S(6)} %copy.95, bf16[1024,4,64]{0,2,1:T(8,128)(2,1)S(1)} %get-tuple-element.573, f32[4,512,1024]{2,1,0:T(8,128)} %fusion.198, f32[4,512,1024]{2,1,0:T(8,128)} %copy-done, f32[4,512]{1,0:T(4,128)S(1)} %dynamic-slice_bitcast_fusion.2, ...), kind=kOutput, calls=%fused_computation.43.clone.1 | convolution fusion | flops 291507200 | bytes 34621444 | tf_op jit(solution)/shard_map/while/body/eval_jaxpr/while/body/eval_jaxpr/hqk,khd->qhd/dot_general | solution.py:137
  556.2 4.3 fusion.201
  560.5 4.5 fusion.198
  565.0 22.7 %fusion.200 = f32[1024,4,64]{0,2,1:T(8,128)} fusion(f32[4,512,1024]{2,1,0:T(8,128)} %fusion.198, f32[4,512,1024]{2,1,0:T(8,128)} %copy-done, f32[4,512]{1,0:T(4,128)S(1)} %dynamic-slice_bitcast_fusion.2, pred[1024]{0:T(1024)(128)(4,1)S(1)} %iota_compare_fusion.5, f32[1024,4,64]{0,2,1:T(8,128)} %get-tuple-element.557, pred[]{:T(512)S(6)} %compare.3, ...), kind=kOutput, calls=%fused_computation.40.clone.1 | convolution fusion | flops 292031488 | bytes 35932164 | tf_op jit(solution)/shard_map/while/body/eval_jaxpr/while/body/eval_jaxpr/hqk,qhd->khd/dot_general | solution.py:140
  587.7 22.1 %fusion.202 = f32[2,512,4,64]{1,3,2,0:T(8,128)} fusion(f32[2,512,4,64]{1,3,2,0:T(8,128)} %get-tuple-element.559, s32[]{:T(128)S(6)} %copy.95, bf16[1024,4,64]{0,2,1:T(8,128)(2,1)S(1)} %get-tuple-element.573, f32[4,512,1024]{2,1,0:T(8,128)} %fusion.198, f32[4,512,1024]{2,1,0:T(8,128)} %copy-done, f32[4,512]{1,0:T(4,128)S(1)} %dynamic-slice_bitcast_fusion.2, ...), kind=kOutput, calls=%fused_computation.43.clone.1 | convolution fusion | flops 291507200 | bytes 34621444 | tf_op jit(solution)/shard_map/while/body/eval_jaxpr/while/body/eval_jaxpr/hqk,khd->qhd/dot_general | solution.py:137
  609.8 1.7 fusion.113
  612.2 3.5 convolution_bitcast_fusion
  616.1 1.7 fusion.114
  619.2 1.7 convolution_bitcast_fusion.2
  623.1 1.7 convolution_bitcast_fusion.1
  624.9 2.1 fusion.120
  627.8 2.7 add_add_fusion
  632.1 5.9 fusion.123
  639.7 6.0 fusion.104
  646.8 3.3 fusion.122
  651.8 13.6 %all-reduce.19 = (f32[256]{0:T(256)S(1)}, f32[256]{0:T(256)S(1)}, f32[1024]{0:T(1024)S(1)}) all-reduce(f32[256]{0:T(256)S(1)} %reduce_sum.200, f32[256]{0:T(256)S(1)} %reduce_sum.202, f32[1024]{0:T(1024)S(1)} %get-tuple-element.402), channel_id=8, replica_groups=mesh['dp'=8,'tensor'=4] {'dp'}, use_global_device_ids=true, to_apply=%region_22.23.clone | all-reduce | flops 1536 | bytes 12288
  667.2 1.7 copy.64
  668.8 21.1 %reduce-scatter.16.cloned.1.call-done = f32[128,256]{0,1:T(8,128)} async-done(((f32[1024,256]{0,1:T(8,128)}), f32[128,256]{0,1:T(8,128)}) %reduce-scatter.16.cloned.1.call-update) | async-done | bytes 131088 | tf_op jit(solution)/shard_map/reduce_scatter | solution.py:277
  689.9 1.7 copy.62
  691.6 37.9 %reduce-scatter.18.cloned.1.call-done = f32[128,256]{0,1:T(8,128)} async-done(((f32[1024,256]{0,1:T(8,128)}), f32[128,256]{0,1:T(8,128)}) %reduce-scatter.18.cloned.1.call-update) | async-done | bytes 131088 | tf_op jit(solution)/shard_map/reduce_scatter | solution.py:278
  729.5 1.7 copy.63
  731.2 77.5 %reduce-scatter.14.cloned.1.call-done = f32[256,1024]{1,0:T(8,128)} async-done(((f32[1024,1024]{1,0:T(8,128)}), f32[256,1024]{1,0:T(8,128)}) %reduce-scatter.14.cloned.1.call-update) | async-done | bytes 1048592 | tf_op jit(solution)/shard_map/reduce_scatter | solution.py:66
  808.6 2.4 fusion.115
  811.0 41.4 %all-reduce.17 = (f32[1024]{0:T(1024)S(1)}, f32[1024]{0:T(1024)S(1)}, f32[1024]{0:T(1024)S(1)}, f32[1024]{0:T(1024)S(1)}, f32[1024]{0:T(1024)S(1)}, /*index=5*/f32[1024]{0:T(1024)S(1)}, f32[1024]{0:T(1024)S(1)}) all-reduce(f32[1024]{0:T(1024)S(1)} %dynamic-update-slice.7, ...), channel_id=1, replica_groups=mesh['dp'=8,'tensor'=4] {'dp','tensor'}, use_global_device_ids=true, to_apply=%add.7 | all-reduce | flops 7168 | bytes 57344
  857.0 7.4 reduce-scatter.26.cloned.1.call-done
  864.4 55.0 %reduce-scatter.24.cloned.1.call-done = f32[128,1024]{1,0:T(8,128)} async-done(((f32[1024,1024]{1,0:T(8,128)}), f32[128,1024]{1,0:T(8,128)}) %reduce-scatter.24.cloned.1.call-update) | async-done | bytes 524304 | tf_op jit(solution)/shard_map/reduce_scatter | solution.py:281
  919.4 39.6 %reduce-scatter.22.cloned.1.call-done = f32[256,128]{1,0:T(8,128)} async-done(((f32[256,1024]{1,0:T(8,128)}), f32[256,128]{1,0:T(8,128)}) %reduce-scatter.22.cloned.1.call-update) | async-done | bytes 131088 | tf_op jit(solution)/shard_map/reduce_scatter | solution.py:280
  (179 shorter events, 44.9 us)
Async XLA Ops:
  7.2 60.5 %all-gather.9.cloned.1.call-start = ((), (), s32[]{:S(2)}) async-start(), calls=%async_computation.10 | async-start | bytes 2621440 | tf_op jit(solution)/shard_map/all_gather | solution.py:54
  7.9 131.8 %all-gather.11.cloned.1.call-start = ((), (), s32[]{:S(2)}) async-start(), calls=%async_computation.11 | async-start | bytes 2621440 | tf_op jit(solution)/shard_map/all_gather | solution.py:228
  21.4 133.4 %all-gather.15.cloned.1.call-start = ((), (), s32[]{:S(2)}) async-start(), calls=%async_computation.13 | async-start | bytes 2359296 | tf_op jit(solution)/shard_map/all_gather | solution.py:196
  49.0 18.7 %copy-start.15 = (bf16[1024,256]{1,0:T(8,128)(2,1)}, bf16[1024,256]{1,0:T(8,128)(2,1)S(1)}, u32[]{:S(2)}) copy-start(bf16[1024,256]{1,0:T(8,128)(2,1)S(1)} %all_gather.67) | copy-start | bytes 1572868
  58.6 12.7 %copy-start.13 = (bf16[1024,256]{1,0:T(8,128)(2,1)}, bf16[1024,256]{1,0:T(8,128)(2,1)S(1)}, u32[]{:S(2)}) copy-start(bf16[1024,256]{1,0:T(8,128)(2,1)S(1)} %all_gather.69) | copy-start | bytes 1572868
  67.7 5.9 copy-start.17
  78.1 2.0 copy-start.19
  82.2 0.8 copy-start.20
  85.1 2.0 copy-start.19
  89.2 0.8 copy-start.20
  90.0 53.2 %copy-start.2 = (bf16[1024,4,64]{0,2,1:T(8,128)(2,1)}, bf16[1024,4,64]{0,2,1:T(8,128)(2,1)S(1)}, u32[]{:S(2)}) copy-start(bf16[1024,4,64]{0,2,1:T(8,128)(2,1)S(1)} %get-tuple-element.601) | copy-start | bytes 1572868
  90.0 8.0 copy-start.25
  90.0 8.2 copy-start.26
  90.0 8.4 copy-start.27
  90.0 8.7 copy-start.28
  90.0 8.9 copy-start.29
  91.9 51.6 %copy-start.8 = (bf16[2,512,4,64]{1,0,3,2:T(2,128)(2,1)}, bf16[2,512,4,64]{1,0,3,2:T(2,128)(2,1)S(1)}, u32[]{:S(2)}) copy-start(bf16[2,512,4,64]{1,0,3,2:T(2,128)(2,1)S(1)} %copy.55) | copy-start | bytes 1572868
  92.9 52.2 %copy-start.21 = (bf16[128]{0:T(256)(128)(2,1)S(1)}, bf16[128]{0:T(256)(128)(2,1)}, u32[]{:S(2)}) copy-start(bf16[128]{0:T(256)(128)(2,1)} %param.34) | copy-start | bytes 772
  92.9 46.8 %all-to-all-start = ((bf16[4,256,256]{1,2,0:T(8,128)(2,1)}), bf16[4,256,256]{1,2,0:T(8,128)(2,1)S(1)}, u32[]{:S(2)}, u32[]{:S(2)}) async-start(bf16[4,256,256]{1,2,0:T(8,128)(2,1)} %copy.56), calls=%async_computation | async-start | bytes 1048576 | tf_op jit(solution)/shard_map/all_to_all | solution.py:227
  98.0 92.8 %all-gather.13.cloned.1.call-start = ((), (), s32[]{:S(2)}) async-start(), calls=%async_computation.12 | async-start | bytes 2621440 | tf_op jit(solution)/shard_map/all_gather | solution.py:54
  139.7 0.8 copy-start.16
  144.5 74.9 %all-gather.17.cloned.1.call-start = ((), (), s32[]{:S(2)}) async-start(), calls=%async_computation.14 | async-start | bytes 2359296 | tf_op jit(solution)/shard_map/all_gather | solution.py:197
  145.1 157.8 %reduce-scatter.10.cloned.1.call-start = ((), (), s32[]{:S(2)}) async-start(), calls=%async_computation.15 | async-start | bytes 5242880 | tf_op jit(solution)/shard_map/reduce_scatter | solution.py:58
  226.0 130.1 %all-gather.19.cloned.1.call-start = ((), (), s32[]{:S(2)}) async-start(), calls=%async_computation.16 | async-start | bytes 2621440 | tf_op jit(solution)/shard_map/all_gather | solution.py:62
  307.8 1.0 copy-start.4
  309.7 134.4 %reduce-scatter.12.cloned.1.call-start = ((), (), s32[]{:S(2)}) async-start(), calls=%async_computation.17 | async-start | bytes 5242880 | tf_op jit(solution)/shard_map/reduce_scatter | solution.py:66
  356.0 8.0 copy-start.23
  362.7 1.3 copy-start.31
  368.3 125.7 %all-gather.21.cloned.1.call-start = ((), (), s32[]{:S(2)}) async-start(), calls=%async_computation.18 | async-start | bytes 2621440 | tf_op jit(solution)/shard_map/all_gather | solution.py:62
  447.7 219.5 %reduce-scatter.20.cloned.1.call-start = ((), (), s32[]{:S(2)}) async-start(), calls=%async_computation.22 | async-start | bytes 1179648 | tf_op jit(solution)/shard_map/reduce_scatter | solution.py:279
  447.8 51.7 %copy-start.3 = (bf16[1024,4,64]{0,2,1:T(8,128)(2,1)S(1)}, bf16[1024,4,64]{0,2,1:T(8,128)(2,1)}, u32[]{:S(2)}) copy-start(bf16[1024,4,64]{0,2,1:T(8,128)(2,1)} %copy-done.2) | copy-start | bytes 1572868
  501.4 3.5 copy-start
  556.2 4.3 copy-start
  611.5 0.8 copy-start.10
  612.2 6.9 copy-start.1
  615.8 74.2 %reduce-scatter.16.cloned.1.call-start = ((), (), s32[]{:S(2)}) async-start(), calls=%async_computation.20 | async-start | bytes 1179648 | tf_op jit(solution)/shard_map/reduce_scatter | solution.py:277
  618.4 0.8 copy-start.7
  620.9 108.6 %reduce-scatter.18.cloned.1.call-start = ((), (), s32[]{:S(2)}) async-start(), calls=%async_computation.21 | async-start | bytes 1179648 | tf_op jit(solution)/shard_map/reduce_scatter | solution.py:278
  622.3 0.8 copy-start.5
  624.8 2.2 copy-start.6
  624.8 2.2 copy-start.14
  624.8 3.0 copy-start.11
  624.8 3.0 copy-start.18
  624.8 183.8 %reduce-scatter.14.cloned.1.call-start = ((), (), s32[]{:S(2)}) async-start(), calls=%async_computation.19 | async-start | bytes 5242880 | tf_op jit(solution)/shard_map/reduce_scatter | solution.py:66
  630.6 1.6 copy-start.24
  630.6 233.8 %reduce-scatter.26.cloned.1.call-start = ((), (), s32[]{:S(2)}) async-start(), calls=%async_computation.25 | async-start | bytes 4718592 | tf_op jit(solution)/shard_map/reduce_scatter | solution.py:282
  638.1 1.6 copy-start.22
  638.1 281.3 %reduce-scatter.24.cloned.1.call-start = ((), (), s32[]{:S(2)}) async-start(), calls=%async_computation.24 | async-start | bytes 4718592 | tf_op jit(solution)/shard_map/reduce_scatter | solution.py:281
  645.7 1.1 copy-start.9
  645.7 5.7 copy-start.30
  645.7 163.0 %copy-start.12 = (f32[256,1024]{1,0:T(8,128)S(1)}, f32[256,1024]{1,0:T(8,128)}, u32[]{:S(2)}) copy-start(f32[256,1024]{1,0:T(8,128)} %get-tuple-element.382) | copy-start | bytes 3145732
  645.7 313.3 %reduce-scatter.22.cloned.1.call-start = ((), (), s32[]{:S(2)}) async-start(), calls=%async_computation.23 | async-start | bytes 1179648 | tf_op jit(solution)/shard_map/reduce_scatter | solution.py:280
Sparse Core Ops, SparseCore 0:
  9.6 48.3 all-gather.8
  59.5 48.2 all-gather.10
  109.8 26.5 all-gather.14
  144.6 46.0 all-gather.12
  192.5 26.8 all-gather.16
  226.1 76.7 reduce-scatter.9
  309.8 46.1 all-gather.18
  368.5 75.5 reduce-scatter.11
  447.8 46.1 all-gather.20
  615.9 34.7 reduce-scatter.19
  653.9 36.0 reduce-scatter.15
  693.5 35.9 reduce-scatter.17
  731.8 76.7 reduce-scatter.13
  812.4 51.9 reduce-scatter.25
  868.2 51.1 reduce-scatter.23
  923.0 35.9 reduce-scatter.21
where the time goes:
time: 976 us; the launch traced here: 966 us
  waiting for transfers between devices  543 us (56%)
  matrix products  181 us (19%)
  blocking collectives  160 us (16%)
  local copies, waits for them, and re-layouts  33.5 us (3%)
  other arithmetic  25.4 us (3%)
  between operations  16.9 us (2%)
    reduce_scatter x2, waiting for transfers between devices, share_grads(): lax.psum_scatter(partial_value, 'tensor', scatter_dimension=0, tiled=True)  153 us
    unnamed x4, blocking collectives  110 us
    all_gather x2, waiting for transfers between devices, whole_grads(): return lax.all_gather(part_rows, 'tensor', axis=0, tiled=True)  92.5 us
    reduce_scatter x1, waiting for transfers between devices, share_rows(): lax.psum_scatter(partial_value, 'tensor', scatter_dimension=0, tiled=True)  76.9 us
    reduce_scatter x1, waiting for transfers between devices, per_device(): lax.psum_scatter(inner_grad, 'dp', scatter_dimension=0, tiled=True)  55 us
    dot_general x2, matrix products, one_block(): jnp.einsum('hqk,qhd->khd', d_scores, q_block, preferred_element_type=jnp....  45.3 us
    dot_general x2, matrix products, one_block(): jnp.einsum('hqk,khd->qhd', d_scores, k_seq, preferred_element_type=jnp.fl...  44.2 us
    reduce_scatter x1, waiting for transfers between devices, per_device(): lax.psum_scatter(output_grad, 'dp', scatter_dimension=1, tiled=True)  39.6 us
  transfers between devices with their start and end apart: 17, of which 12 were waited for; matrix products, arithmetic and copies ran while one was open for 8% of the time, Pallas kernels for 0%

commit v1 on v0

v1 whole, which is shorter than its diff:
```python
import jax
import jax.numpy as jnp
from jax import lax
from jax.experimental import pallas as pl
from jax.experimental.pallas import tpu as pltpu
from jax.sharding import PartitionSpec as P

HEAD_DIM = 64


inv_root2 = 0.7071067811865476
inv_root2pi = 0.3989422804014327
norm_eps = 1e-06


def gelu_cdf(values):
    return 0.5 * (1.0 + jax.scipy.special.erf(values * inv_root2))


def row_norm(resid_rows, norm_gain, norm_shift):
    center = resid_rows - jnp.mean(resid_rows, axis=-1, keepdims=True)
    inverse = lax.rsqrt(jnp.mean(center * center, axis=-1, keepdims=True) + norm_eps)
    return center * inverse * norm_gain + norm_shift


def norm_back(resid_rows, norm_gain, upstream):
    center = resid_rows - jnp.mean(resid_rows, axis=-1, keepdims=True)
    inverse = lax.rsqrt(jnp.mean(center * center, axis=-1, keepdims=True) + norm_eps)
    normed = center * inverse
    scaled_up = upstream * norm_gain
    d_resid = inverse * (
        scaled_up
        - jnp.mean(scaled_up, axis=-1, keepdims=True)
        - normed * jnp.mean(scaled_up * normed, axis=-1, keepdims=True)
    )
    return (d_resid, jnp.sum(upstream * normed, axis=0), jnp.sum(upstream, axis=0))


def dense(left, right):
    return jnp.dot(left, right, preferred_element_type=jnp.float32)


def dense_tn(left, right):
    return lax.dot_general(
        left, right, (((0,), (0,)), ((), ())), preferred_element_type=jnp.float32
    )


def dense_nt(left, right):
    return lax.dot_general(
        left, right, (((1,), (1,)), ((), ())), preferred_element_type=jnp.float32
    )


def whole_rows(part_rows):
    return lax.all_gather(part_rows, "tensor", axis=0, tiled=True)


def share_rows(partial_value):
    partial_b = partial_value.astype(jnp.bfloat16)
    return lax.psum_scatter(partial_b, "tensor", scatter_dimension=0, tiled=True).astype(jnp.float32)


def share_grad(partial_value, axis):
    partial_b = partial_value.astype(jnp.bfloat16)
    return lax.psum_scatter(partial_b, "dp", scatter_dimension=axis, tiled=True).astype(jnp.float32)


def gather_vectors(vectors, biases):
    mesh_dp, mesh_tensor = lax.axis_size("dp"), lax.axis_size("tensor")
    parts = list(vectors) + [bias.astype(jnp.float32) for bias in biases]
    packed = jnp.concatenate(parts)[None, :]
    every = lax.all_gather(packed, ("dp", "tensor"), axis=0, tiled=True)
    full, start = [], 0
    for part in vectors:
        full.append(every[:, start : start + part.shape[0]].reshape(-1))
        start += part.shape[0]
    own = lax.dynamic_index_in_dim(
        every.reshape(mesh_dp, mesh_tensor, -1), lax.axis_index("tensor"), 1, keepdims=False
    )
    for part in biases:
        full.append(own[:, start : start + part.shape[0]].reshape(-1))
        start += part.shape[0]
    return full


def share_vectors(vectors, biases):
    mesh_dp, mesh_tensor = lax.axis_size("dp"), lax.axis_size("tensor")
    parts = [part.reshape(mesh_dp, mesh_tensor, -1) for part in vectors]
    packed = jnp.concatenate(parts, axis=2)
    width = packed.shape[2]
    rows = [packed.reshape(mesh_dp, -1)] + [part.reshape(mesh_dp, -1) for part in biases]
    mine = lax.psum_scatter(jnp.concatenate(rows, axis=1), "dp", scatter_dimension=0, tiled=True)[0]
    own = lax.psum_scatter(
        mine[: mesh_tensor * width].reshape(mesh_tensor, width),
        "tensor",
        scatter_dimension=0,
        tiled=True,
    )[0]
    sent = list(own.reshape(len(vectors), -1))
    start = mesh_tensor * width
    for part in biases:
        size = part.shape[0] // mesh_dp
        sent.append(mine[start : start + size])
        start += size
    return sent


def attn_fwd_kernel(len_ref, q_ref, k_ref, v_ref, ctx_ref, p_ref):
    seq_len = q_ref.shape[0]
    rows = min(256, seq_len)
    length = len_ref[pl.program_id(0)]
    spot = lax.broadcasted_iota(jnp.int32, (1, seq_len), 1)
    bias = jnp.where(spot < length, 0.0, -jnp.inf).astype(jnp.float32)
    scale = HEAD_DIM ** (-0.5)

    def step(i, carry):
        here = pl.ds(pl.multiple_of(i * rows, rows), rows)
        parts = []
        for h in range(2):
            cols = slice(h * HEAD_DIM, (h + 1) * HEAD_DIM)
            scores = dense_nt(q_ref[here, cols], k_ref[:, cols]) * scale + bias
            top = jnp.max(scores, axis=-1, keepdims=True)
            grown = jnp.exp(scores - top)
            total = jnp.sum(grown, axis=-1, keepdims=True)
            probs = (grown * (1.0 / total)).astype(jnp.bfloat16)
            p_ref[h, here, :] = probs
            parts.append(dense(probs, v_ref[:, cols]))
        ctx_ref[here, :] = jnp.concatenate(parts, axis=1).astype(jnp.bfloat16)
        return carry

    lax.fori_loop(0, seq_len // rows, step, 0)


def attention_fwd(q_rows, k_rows, v_rows, lengths):
    seqs = lengths.shape[0]
    seq_len = q_rows.shape[0] // seqs
    pairs = q_rows.shape[1] // (2 * HEAD_DIM)
    tile = pl.BlockSpec((seq_len, 2 * HEAD_DIM), lambda s, h, ln: (s, h))
    return pl.pallas_call(
        attn_fwd_kernel,
        grid_spec=pltpu.PrefetchScalarGridSpec(
            num_scalar_prefetch=1,
            grid=(seqs, pairs),
            in_specs=[tile, tile, tile],
            out_specs=[
                tile,
                pl.BlockSpec((2, seq_len, seq_len), lambda s, h, ln: (s * pairs + h, 0, 0)),
            ],
        ),
        out_shape=[
            jax.ShapeDtypeStruct(q_rows.shape, jnp.bfloat16),
            jax.ShapeDtypeStruct((seqs * pairs * 2, seq_len, seq_len), jnp.bfloat16),
        ],
        compiler_params=pltpu.CompilerParams(vmem_limit_bytes=48 << 20),
        name="attn_fwd",
    )(lengths, q_rows, k_rows, v_rows)


def attn_bwd_kernel(q_ref, k_ref, v_ref, p_ref, g_ref, dq_ref, dk_ref, dv_ref, qb_ref, vb_ref, dk_sum, dv_sum):
    seq_len = q_ref.shape[0]
    rows = min(256, seq_len)
    scale = HEAD_DIM ** (-0.5)
    dk_sum[...] = jnp.zeros_like(dk_sum)
    dv_sum[...] = jnp.zeros_like(dv_sum)

    def step(i, total):
        here = pl.ds(pl.multiple_of(i * rows, rows), rows)
        parts = []
        for h in range(2):
            cols = slice(h * HEAD_DIM, (h + 1) * HEAD_DIM)
            grad = g_ref[here, cols]
            probs_b = p_ref[h, here, :]
            probs = probs_b.astype(jnp.float32)
            d_probs = dense_nt(grad, v_ref[:, cols])
            inner = jnp.sum(probs * d_probs, axis=-1, keepdims=True)
            d_scores = (probs * (d_probs - inner)).astype(jnp.bfloat16)
            parts.append(dense(d_scores, k_ref[:, cols]) * scale)
            dv_sum[cols, :] += dense_tn(grad, probs_b)
            dk_sum[cols, :] += dense_tn(q_ref[here, cols], d_scores)
        d_query = jnp.concatenate(parts, axis=1)
        dq_ref[here, :] = d_query.astype(jnp.bfloat16)
        return total + jnp.sum(d_query, axis=0, keepdims=True)

    qb_ref[0] = lax.fori_loop(0, seq_len // rows, step, jnp.zeros((1, 2 * HEAD_DIM), jnp.float32))
    dk_ref[...] = (jnp.transpose(dk_sum[...]) * scale).astype(jnp.bfloat16)
    d_value = jnp.transpose(dv_sum[...])
    dv_ref[...] = d_value.astype(jnp.bfloat16)
    vb_ref[0] = jnp.sum(d_value, axis=0, keepdims=True)


def attention_bwd(q_rows, k_rows, v_rows, probs_b, d_context, seqs):
    seq_len = q_rows.shape[0] // seqs
    wide = 2 * HEAD_DIM
    pairs = q_rows.shape[1] // wide
    tile = pl.BlockSpec((seq_len, wide), lambda s, h: (s, h))
    line = pl.BlockSpec((1, 1, wide), lambda s, h: (s, 0, h))
    grads = jax.ShapeDtypeStruct(q_rows.shape, jnp.bfloat16)
    sums = jax.ShapeDtypeStruct((seqs, 1, q_rows.shape[1]), jnp.float32)
    dq, dk, dv, qb, vb = pl.pallas_call(
        attn_bwd_kernel,
        grid=(seqs, pairs),
        in_specs=[
            tile,
            tile,
            tile,
            pl.BlockSpec((2, seq_len, seq_len), lambda s, h: (s * pairs + h, 0, 0)),
            tile,
        ],
        out_specs=[tile, tile, tile, line, line],
        out_shape=[grads, grads, grads, sums, sums],
        scratch_shapes=[
            pltpu.VMEM((wide, seq_len), jnp.float32),
            pltpu.VMEM((wide, seq_len), jnp.float32),
        ],
        compiler_params=pltpu.CompilerParams(vmem_limit_bytes=48 << 20),
        name="attn_bwd",
    )(q_rows, k_rows, v_rows, probs_b, d_context)
    return dq, dk, dv, jnp.sum(qb, axis=(0, 1)), jnp.sum(vb, axis=(0, 1))


def per_device(
    block_input,
    lengths,
    query_weight,
    key_weight,
    value_weight,
    query_bias,
    value_bias,
    output_weight,
    output_bias,
    first_gain,
    first_shift,
    inner_weight,
    inner_bias,
    outer_weight,
    outer_bias,
    second_gain,
    second_shift,
    cotangent,
):
    seq_rows = whole_rows(block_input)
    (
        full_obias,
        full_gain1,
        full_shift1,
        full_bias2,
        full_gain2,
        full_shift2,
        bias_query,
        bias_value,
        bias_inner,
    ) = gather_vectors(
        (output_bias, first_gain, first_shift, outer_bias, second_gain, second_shift),
        (query_bias, value_bias, inner_bias),
    )
    wide_query = lax.all_gather(query_weight, "dp", axis=0, tiled=True)
    wide_key = lax.all_gather(key_weight, "dp", axis=0, tiled=True)
    wide_value = lax.all_gather(value_weight, "dp", axis=0, tiled=True)
    wide_output = lax.all_gather(output_weight, "dp", axis=1, tiled=True)
    wide_inner = lax.all_gather(inner_weight, "dp", axis=0, tiled=True)
    wide_outer = lax.all_gather(outer_weight, "dp", axis=1, tiled=True)
    q_rows = (dense(seq_rows, wide_query) + bias_query).astype(jnp.bfloat16)
    k_rows = dense(seq_rows, wide_key).astype(jnp.bfloat16)
    v_rows = (dense(seq_rows, wide_value) + bias_value).astype(jnp.bfloat16)
    context, probs_b = attention_fwd(q_rows, k_rows, v_rows, lengths)
    own_context = lax.all_to_all(context, "tensor", split_axis=0, concat_axis=1, tiled=True)
    all_output = lax.all_gather(wide_output, "tensor", axis=0, tiled=True)
    attn_sum = dense(own_context, all_output)
    resid_one = block_input.astype(jnp.float32) + attn_sum + full_obias
    middle = row_norm(resid_one, full_gain1, full_shift1)
    middle_rows = whole_rows(middle.astype(jnp.bfloat16))
    pre_act = dense(middle_rows, wide_inner) + bias_inner
    hidden_b = (pre_act * gelu_cdf(pre_act)).astype(jnp.bfloat16)
    resid_two = middle + share_rows(dense(hidden_b, wide_outer)) + full_bias2
    block_output = row_norm(resid_two, full_gain2, full_shift2).astype(jnp.bfloat16)
    d_resid2, gain2_grad, shift2_grad = norm_back(
        resid_two, full_gain2, cotangent.astype(jnp.float32)
    )
    ffn_rows = whole_rows(d_resid2.astype(jnp.bfloat16))
    gelu_slope = gelu_cdf(pre_act) + pre_act * inv_root2pi * jnp.exp(-0.5 * pre_act * pre_act)
    d_pre = dense_nt(ffn_rows, wide_outer) * gelu_slope
    d_pre_b = d_pre.astype(jnp.bfloat16)
    ibias_grad = jnp.sum(d_pre, axis=0)
    d_middle = share_rows(dense_nt(d_pre_b, wide_inner)) + d_resid2
    sent_outer = share_grad(dense_tn(hidden_b, ffn_rows), 1)
    sent_inner = share_grad(dense_tn(middle_rows, d_pre_b), 0)
    d_resid1, gain1_grad, shift1_grad = norm_back(resid_one, full_gain1, d_middle)
    d_attn = d_resid1.astype(jnp.bfloat16)
    own_d_context = dense_nt(d_attn, all_output).astype(jnp.bfloat16)
    d_context = lax.all_to_all(own_d_context, "tensor", split_axis=1, concat_axis=0, tiled=True)
    attn_rows = whole_rows(d_attn)
    sent_output = share_grad(dense_tn(context, attn_rows), 1)
    dq_b, dk_b, dv_b, qbias_grad, vbias_grad = attention_bwd(
        q_rows, k_rows, v_rows, probs_b, d_context, lengths.shape[0]
    )
    input_grad = (
        share_rows(
            dense_nt(dq_b, wide_query) + dense_nt(dk_b, wide_key) + dense_nt(dv_b, wide_value)
        )
        + d_resid1
    )
    sent_query = share_grad(dense_tn(seq_rows, dq_b), 0)
    sent_key = share_grad(dense_tn(seq_rows, dk_b), 0)
    sent_value = share_grad(dense_tn(seq_rows, dv_b), 0)
    (
        sent_obias,
        sent_gain1,
        sent_shift1,
        sent_bias2,
        sent_gain2,
        sent_shift2,
        sent_qbias,
        sent_vbias,
        sent_ibias,
    ) = share_vectors(
        (
            jnp.sum(d_resid1, axis=0),
            gain1_grad,
            shift1_grad,
            jnp.sum(d_resid2, axis=0),
            gain2_grad,
            shift2_grad,
        ),
        (qbias_grad, vbias_grad, ibias_grad),
    )
    return (
        block_output,
        input_grad,
        sent_query,
        sent_key,
        sent_value,
        sent_qbias,
        sent_vbias,
        sent_output,
        sent_obias,
        sent_gain1,
        sent_shift1,
        sent_inner,
        sent_ibias,
        sent_outer,
        sent_bias2,
        sent_gain2,
        sent_shift2,
    )


def solution(mesh):
    return jax.shard_map(
        per_device,
        mesh=mesh,
        in_specs=(
            P(("dp", "tensor"), None),
            P("dp"),
            P("dp", "tensor"),
            P("dp", "tensor"),
            P("dp", "tensor"),
            P(("tensor", "dp")),
            P(("tensor", "dp")),
            P("tensor", "dp"),
            P(("dp", "tensor")),
            P(("dp", "tensor")),
            P(("dp", "tensor")),
            P("dp", "tensor"),
            P(("tensor", "dp")),
            P("tensor", "dp"),
            P(("dp", "tensor")),
            P(("dp", "tensor")),
            P(("dp", "tensor")),
            P(("dp", "tensor"), None),
        ),
        out_specs=(
            P(("dp", "tensor"), None),
            P(("dp", "tensor"), None),
            P("dp", "tensor"),
            P("dp", "tensor"),
            P("dp", "tensor"),
            P(("tensor", "dp")),
            P(("tensor", "dp")),
            P("tensor", "dp"),
            P(("dp", "tensor")),
            P(("dp", "tensor")),
            P(("dp", "tensor")),
            P("dp", "tensor"),
            P(("tensor", "dp")),
            P("tensor", "dp"),
            P(("dp", "tensor")),
            P(("dp", "tensor")),
            P(("dp", "tensor")),
        ),
        check_vma=False,
    )
```

time: 976 us -> 746 us (0.76)
  waiting for transfers between devices: 543 us -> 410 us
  matrix products: 181 us -> 58.3 us
  Pallas kernels: 0 us -> 29.4 us
  blocking collectives: 160 us -> 179 us
    reduce_scatter x9 -> x4, waiting for transfers between devices: 391 us -> 172 us  [the longest x3 130 us: share_rows(): lax.psum_scatter(partial_b, 'tensor', scatter_dimension=0, tiled=True)]
    dot_general x14 -> x0, matrix products: 116 us -> none  [the longest x2 45.3 us: one_block(): jnp.einsum('hqk,qhd->khd', d_scores, q_block, preferred_element_type=jnp....]
    unnamed x16 -> x21, waiting for transfers between devices: 2.11 us -> 113 us
    all_gather x4 -> x2, waiting for transfers between devices: 114 us -> 21.2 us  [the longest x1 21.2 us: per_device(): wide_outer = lax.all_gather(outer_weight, 'dp', axis=1, tiled=True)]
    unnamed x4 -> x2, blocking collectives: 110 us -> 34.7 us
    all_gather x5, blocking collectives: 50.8 us -> 112 us  [the longest x1 71.2 us: gather_vectors(): every = lax.all_gather(packed, ('dp', 'tensor'), axis=0, tiled=True)]
    all_gather x2 -> x4, waiting for transfers between devices: 36 us -> 88.4 us  [whole_rows(): return lax.all_gather(part_rows, 'tensor', axis=0, tiled=True)]
    all_to_all x0 -> x1, blocking collectives: none -> 31.9 us  [per_device(): lax.all_to_all(own_d_context, 'tensor', split_axis=1, concat_axis=0, tile...]
  transfers between devices with their start and end apart: 17 -> 17, of which waited for: 12 -> 12; matrix products, arithmetic and copies ran while one was open for 8% -> 10% of each run, Pallas kernels for 0% -> 4%
where the time goes in v1:
time: 746 us; the launch traced here: 745 us
  waiting for transfers between devices  410 us (55%)
  blocking collectives  179 us (24%)
  matrix products  58.3 us (8%)
  local copies, waits for them, and re-layouts  33.1 us (4%)
  Pallas kernels  29.4 us (4%)
  other arithmetic  15.7 us (2%)
  between operations  15.1 us (2%)
    reduce_scatter x3, waiting for transfers between devices, share_rows(): lax.psum_scatter(partial_b, 'tensor', scatter_dimension=0, tiled=True)  130 us
    unnamed x21, waiting for transfers between devices  113 us
    all_gather x4, waiting for transfers between devices, whole_rows(): return lax.all_gather(part_rows, 'tensor', axis=0, tiled=True)  88.4 us
    all_gather x1, blocking collectives, gather_vectors(): every = lax.all_gather(packed, ('dp', 'tensor'), axis=0, tiled=True)  71.2 us
    reduce_scatter x1, waiting for transfers between devices, share_grad(): lax.psum_scatter(partial_b, 'dp', scatter_dimension=axis, tiled=True)  42.5 us
    unnamed x2, blocking collectives  34.7 us
    all_to_all x1, blocking collectives, per_device(): lax.all_to_all(own_d_context, 'tensor', split_axis=1, concat_axis=0, tile...  31.9 us
    unnamed x68, local copies, waits for them, and re-layouts  23.3 us
  transfers between devices with their start and end apart: 17, of which 12 were waited for; matrix products, arithmetic and copies ran while one was open for 10% of the time, Pallas kernels for 4%

profile of v1, /device:TPU:0, one launch (start us, length us, event | category | flops | bytes accessed | tf_op | source)
XLA Modules:
  0.0 744.9 jit_solution(1178571504409327014)
XLA Ops:
  8.0 13.4 %all_gather.41 = bf16[256,1024]{1,0:T(8,128)(2,1)} all-gather(bf16[256,128]{1,0:T(8,128)(2,1)} %param.25), channel_id=1, replica_groups=mesh['dp'=8,'tensor'=4] {'dp'}, dimensions={1}, use_global_device_ids=true | all-gather | bytes 589824 | tf_op jit(solution)/shard_map/all_gather | solution.py:260
  22.2 2.2 concatenate.9
  24.4 71.2 %all-gather.1 = f32[32,1,384]{2,1,0:T(1,128)S(1)} all-gather(f32[1,1,384]{2,1,0:T(1,128)S(1)} %reshape.160), channel_id=2, replica_groups=mesh['dp'=8,'tensor'=4] {'dp','tensor'}, dimensions={0}, use_global_device_ids=true | all-gather | bytes 50688 | tf_op jit(solution)/shard_map/all_gather | solution.py:73
  96.7 9.0 %all_gather.37 = bf16[1024,256]{1,0:T(8,128)(2,1)S(1)} all-gather(bf16[128,256]{1,0:T(8,128)(2,1)S(1)} %copy-done.18), channel_id=1, replica_groups=mesh['dp'=8,'tensor'=4] {'dp'}, dimensions={0}, use_global_device_ids=true | all-gather | bytes 589824 | tf_op jit(solution)/shard_map/all_gather | solution.py:257
  105.7 9.7 %all_gather.40 = bf16[1024,256]{1,0:T(8,128)(2,1)S(1)} all-gather(bf16[128,256]{1,0:T(8,128)(2,1)S(1)} %copy-done.19), channel_id=1, replica_groups=mesh['dp'=8,'tensor'=4] {'dp'}, dimensions={0}, use_global_device_ids=true | all-gather | bytes 589824 | tf_op jit(solution)/shard_map/all_gather | solution.py:259
  115.4 9.0 %all_gather.39 = bf16[1024,256]{1,0:T(8,128)(2,1)S(1)} all-gather(bf16[128,256]{1,0:T(8,128)(2,1)S(1)} %copy-done.20), channel_id=1, replica_groups=mesh['dp'=8,'tensor'=4] {'dp'}, dimensions={0}, use_global_device_ids=true | all-gather | bytes 589824 | tf_op jit(solution)/shard_map/all_gather | solution.py:258
  124.3 0.8 copy-done.12
  125.1 2.4 convolution_convert_fusion.9.k_ref
  129.1 14.3 %attn_fwd.1 = (bf16[1024,256]{1,0:T(8,128)(2,1)S(1)}, bf16[4,1024,1024]{2,1,0:T(8,128)(2,1)}) custom-call(s32[1]{0:T(128)S(6)} %copy.69.len_ref, bf16[1024,256]{1,0:T(8,128)(2,1)S(1)} %fusion.8.q_ref, bf16[1024,256]{1,0:T(8,128)(2,1)S(1)} %convolution_convert_fusion.9.k_ref, bf16[1024,256]{1,0:T(8,128)(2,1)S(1)} %fusion.9.v_ref), custom_call_target="tpu_custom_call" | custom-call | tf_op jit(solution)/shard_map/attn_fwd/pallas_call | solution.py:140
  143.4 1.0 copy.44
  144.4 3.5 all-to-all-start
  148.2 14.9 %all-to-all-done = bf16[4,256,256]{1,2,0:T(8,128)(2,1)S(1)} async-done(((bf16[4,256,256]{1,2,0:T(8,128)(2,1)}), bf16[4,256,256]{1,2,0:T(8,128)(2,1)S(1)}, u32[]{:S(2)}, u32[]{:S(2)}) %all-to-all-start) | async-done | bytes 524320 | tf_op jit(solution)/shard_map/all_to_all | solution.py:267
  163.9 2.7 fusion.27
  166.8 1.1 fusion.19
  168.6 43.4 %all-gather.14.cloned.1.call-done = bf16[1024,1024]{1,0:T(8,128)(2,1)} async-done(((bf16[256,1024]{1,0:T(8,128)(2,1)}), bf16[1024,1024]{1,0:T(8,128)(2,1)}) %all-gather.14.cloned.1.call-update) | async-done | bytes 2097168 | tf_op jit(solution)/shard_map/all_gather | solution.py:56
  212.0 7.5 %multiply_convert_fusion = (bf16[1024,1024]{1,0:T(8,128)(2,1)}, f32[1024,1024]{1,0:T(8,128)}) fusion(f32[1024]{0:T(1024)S(1)} %slice_bitcast_fusion, bf16[1024,1024]{1,0:T(8,128)(2,1)} %all-gather.14.cloned.1.call-done, bf16[1024,1024]{1,0:T(8,128)(2,1)} %all-gather.16.cloned.1.call-done), kind=kOutput, calls=%fused_computation.6 | convolution fusion | flops 2153775104 | bytes 10489856 | tf_op jit(solution)/shard_map/dot_general | solution.py:40
  219.5 21.2 %all-gather.18.cloned.1.call-done = bf16[1024,1024]{1,0:T(8,128)(2,1)} async-done(((bf16[1024,128]{1,0:T(8,128)(2,1)}), bf16[1024,1024]{1,0:T(8,128)(2,1)}) %all-gather.18.cloned.1.call-update) | async-done | bytes 2097168 | tf_op jit(solution)/shard_map/all_gather | solution.py:262
  240.7 5.9 convolution_convert_fusion.3
  247.1 43.3 %reduce-scatter.20.cloned.1.call-done = bf16[256,1024]{1,0:T(8,128)(2,1)} async-done(((bf16[1024,1024]{1,0:T(8,128)(2,1)}), bf16[256,1024]{1,0:T(8,128)(2,1)}) %reduce-scatter.20.cloned.1.call-update) | async-done | bytes 524304 | tf_op jit(solution)/shard_map/reduce_scatter | solution.py:61
  290.4 1.5 fusion.24
  292.8 1.8 fusion.22
  294.6 45.0 %all-gather.20.cloned.1.call-done = bf16[1024,1024]{1,0:T(8,128)(2,1)} async-done(((bf16[256,1024]{1,0:T(8,128)(2,1)}), bf16[1024,1024]{1,0:T(8,128)(2,1)}) %all-gather.20.cloned.1.call-update) | async-done | bytes 2097168 | tf_op jit(solution)/shard_map/all_gather | solution.py:56
  339.6 6.6 fusion.28
  346.2 1.3 copy-done.24
  347.6 3.7 convolution_convert_fusion.2
  351.3 42.5 %reduce-scatter.22.cloned.1.call-done = bf16[256,1024]{1,0:T(8,128)(2,1)} async-done(((bf16[1024,1024]{1,0:T(8,128)(2,1)}), bf16[256,1024]{1,0:T(8,128)(2,1)}) %reduce-scatter.22.cloned.1.call-update) | async-done | bytes 524304 | tf_op jit(solution)/shard_map/reduce_scatter | solution.py:61
  393.9 2.1 multiply_reduce_fusion
  396.4 1.0 copy-done.5
  397.4 0.9 convert_element_type.125
  398.3 5.9 convolution_convert_fusion
  404.2 4.0 copy.57
  408.3 5.9 convolution_convert_fusion.1
  415.3 2.3 convolution_convert_fusion.8
  417.7 31.9 %all_to_all.38 = bf16[256,4,256]{2,0,1:T(8,128)(2,1)S(1)} all-to-all(bf16[256,4,256]{2,0,1:T(8,128)(2,1)S(1)} %bitcast.94), channel_id=1, replica_groups=mesh['dp'=8,'tensor'=4] {'tensor'}, dimensions={1} | all-to-all | bytes 1048576 | tf_op jit(solution)/shard_map/all_to_all | solution.py:291
  449.6 15.1 %attn_bwd.1 = (bf16[1024,256]{1,0:T(8,128)(2,1)S(1)}, bf16[1024,256]{1,0:T(8,128)(2,1)S(1)}, bf16[1024,256]{1,0:T(8,128)(2,1)S(1)}, f32[1,1,256]{2,1,0:T(1,128)S(1)}, f32[1,1,256]{2,1,0:T(1,128)S(1)}) custom-call(bf16[1024,256]{1,0:T(8,128)(2,1)S(1)} %fusion.8.q_ref, bf16[1024,256]{1,0:T(8,128)(2,1)S(1)} %convolution_convert_fusion.9.k_ref, ...), custom_call_target="tpu_custom_call" | custom-call | tf_op jit(solution)/shard_map/attn_bwd/pallas_call | solution.py:200
  465.4 1.0 copy.49
  466.5 2.4 fusion.11
  468.9 1.0 copy.51
  470.0 2.4 fusion.12
  472.4 1.0 copy.53
  473.5 2.7 fusion.30
  476.2 2.7 convolution_convert_fusion.4
  478.9 1.0 copy.55
  481.0 1.3 copy-done.4
  482.3 2.2 add_convert_fusion
  486.5 11.0 %reduce-scatter.36.cloned.1.call-done = bf16[128,1024]{1,0:T(8,128)(2,1)} async-done(((bf16[1024,1024]{1,0:T(8,128)(2,1)}), bf16[128,1024]{1,0:T(8,128)(2,1)}) %reduce-scatter.36.cloned.1.call-update) | async-done | bytes 262160
  497.5 1.1 copy.58
  498.6 0.8 convert_element_type.143
  499.4 42.5 %reduce-scatter.26.cloned.1.call-done = bf16[128,1024]{1,0:T(8,128)(2,1)} async-done(((bf16[1024,1024]{1,0:T(8,128)(2,1)}), bf16[128,1024]{1,0:T(8,128)(2,1)}) %reduce-scatter.26.cloned.1.call-update) | async-done | bytes 262160 | tf_op jit(solution)/shard_map/reduce_scatter | solution.py:66
  541.9 1.8 convert_element_type.141
  546.3 23.0 %all-reduce = f32[8,960]{1,0:T(8,128)S(1)} all-reduce(f32[8,960]{1,0:T(8,128)S(1)} %pad_maximum_fusion), channel_id=9, replica_groups=mesh['dp'=8,'tensor'=4] {'dp'}, use_global_device_ids=true, to_apply=%region_21.22.clone | all-reduce | flops 7680 | bytes 61440
  570.1 11.7 %all-reduce.1 = f32[4,192]{1,0:T(4,128)S(1)} all-reduce(f32[4,192]{1,0:T(4,128)S(1)} %reshape.157), channel_id=11, replica_groups=mesh['dp'=8,'tensor'=4] {'tensor'}, use_global_device_ids=true, to_apply=%region_23.24.clone | all-reduce | flops 768 | bytes 6144
  581.7 1.2 dynamic-slice_bitcast_fusion.3
  583.0 1.2 dynamic-slice_bitcast_fusion.7
  584.2 1.3 dynamic-slice_bitcast_fusion
  585.5 0.9 copy.50
  587.2 29.1 %reduce-scatter.30.cloned.1.call-done = bf16[128,256]{1,0:T(8,128)(2,1)} async-done(((bf16[1024,256]{1,0:T(8,128)(2,1)}), bf16[128,256]{1,0:T(8,128)(2,1)}) %reduce-scatter.30.cloned.1.call-update) | async-done | bytes 65552
  616.3 0.9 copy.52
  618.0 35.4 %reduce-scatter.32.cloned.1.call-done = bf16[128,256]{1,0:T(8,128)(2,1)} async-done(((bf16[1024,256]{1,0:T(8,128)(2,1)}), bf16[128,256]{1,0:T(8,128)(2,1)}) %reduce-scatter.32.cloned.1.call-update) | async-done | bytes 65552
  653.4 0.9 copy.54
  655.1 35.3 %reduce-scatter.34.cloned.1.call-done = bf16[128,256]{1,0:T(8,128)(2,1)} async-done(((bf16[1024,256]{1,0:T(8,128)(2,1)}), bf16[128,256]{1,0:T(8,128)(2,1)}) %reduce-scatter.34.cloned.1.call-update) | async-done | bytes 65552
  690.4 0.9 copy.56
  692.0 44.2 %reduce-scatter.24.cloned.1.call-done = bf16[256,1024]{1,0:T(8,128)(2,1)} async-done(((bf16[1024,1024]{1,0:T(8,128)(2,1)}), bf16[256,1024]{1,0:T(8,128)(2,1)}) %reduce-scatter.24.cloned.1.call-update) | async-done | bytes 524304 | tf_op jit(solution)/shard_map/reduce_scatter | solution.py:61
  736.2 2.1 convert_add_fusion
  (138 shorter events, 18.6 us)
Async XLA Ops:
  7.2 89.5 %copy-start.18 = (bf16[128,256]{1,0:T(8,128)(2,1)S(1)}, bf16[128,256]{1,0:T(8,128)(2,1)}, u32[]{:S(2)}) copy-start(bf16[128,256]{1,0:T(8,128)(2,1)} %param.20) | copy-start | bytes 196612
  7.2 98.5 %copy-start.19 = (bf16[128,256]{1,0:T(8,128)(2,1)S(1)}, bf16[128,256]{1,0:T(8,128)(2,1)}, u32[]{:S(2)}) copy-start(bf16[128,256]{1,0:T(8,128)(2,1)} %param.22) | copy-start | bytes 196612
  7.2 108.2 %copy-start.20 = (bf16[128,256]{1,0:T(8,128)(2,1)S(1)}, bf16[128,256]{1,0:T(8,128)(2,1)}, u32[]{:S(2)}) copy-start(bf16[128,256]{1,0:T(8,128)(2,1)} %param.21) | copy-start | bytes 196612
  7.2 117.1 %all-gather.10.cloned.1.call-start = ((), (), s32[]{:S(2)}) async-start(), calls=%async_computation.11 | async-start | bytes 2621440 | tf_op jit(solution)/shard_map/all_gather | solution.py:56
  8.0 140.3 %all-gather.12.cloned.1.call-start = ((), (), s32[]{:S(2)}) async-start(), calls=%async_computation.12 | async-start | bytes 2621440 | tf_op jit(solution)/shard_map/all_gather | solution.py:268
  21.4 147.2 %all-gather.16.cloned.1.call-start = ((), (), s32[]{:S(2)}) async-start(), calls=%async_computation.14 | async-start | bytes 2359296 | tf_op jit(solution)/shard_map/all_gather | solution.py:261
  105.7 21.9 %copy-start.10 = (bf16[1024,256]{1,0:T(8,128)(2,1)}, bf16[1024,256]{1,0:T(8,128)(2,1)S(1)}, u32[]{:S(2)}) copy-start(bf16[1024,256]{1,0:T(8,128)(2,1)S(1)} %all_gather.37) | copy-start | bytes 1572868
  115.4 13.0 %copy-start.8 = (bf16[1024,256]{1,0:T(8,128)(2,1)}, bf16[1024,256]{1,0:T(8,128)(2,1)S(1)}, u32[]{:S(2)}) copy-start(bf16[1024,256]{1,0:T(8,128)(2,1)S(1)} %all_gather.40) | copy-start | bytes 1572868
  124.3 0.8 copy-start.12
  125.1 2.5 copy-start.2
  143.4 23.2 %copy-start = (bf16[1024,256]{1,0:T(8,128)(2,1)}, bf16[1024,256]{1,0:T(8,128)(2,1)S(1)}, u32[]{:S(2)}) copy-start(bf16[1024,256]{1,0:T(8,128)(2,1)S(1)} %get-tuple-element.24) | copy-start | bytes 1572868
  144.4 18.7 %all-to-all-start = ((bf16[4,256,256]{1,2,0:T(8,128)(2,1)}), bf16[4,256,256]{1,2,0:T(8,128)(2,1)S(1)}, u32[]{:S(2)}, u32[]{:S(2)}) async-start(bf16[4,256,256]{1,2,0:T(8,128)(2,1)} %copy.44), calls=%async_computation | async-start | bytes 1048576 | tf_op jit(solution)/shard_map/all_to_all | solution.py:267
  147.9 64.1 %all-gather.14.cloned.1.call-start = ((), (), s32[]{:S(2)}) async-start(), calls=%async_computation.13 | async-start | bytes 2621440 | tf_op jit(solution)/shard_map/all_gather | solution.py:56
  163.1 0.8 copy-start.15
  167.9 72.7 %all-gather.18.cloned.1.call-start = ((), (), s32[]{:S(2)}) async-start(), calls=%async_computation.15 | async-start | bytes 2359296 | tf_op jit(solution)/shard_map/all_gather | solution.py:262
  168.5 121.9 %reduce-scatter.20.cloned.1.call-start = ((), (), s32[]{:S(2)}) async-start(), calls=%async_computation.16 | async-start | bytes 2621440 | tf_op jit(solution)/shard_map/reduce_scatter | solution.py:61
  246.6 45.6 %copy-start.16 = (bf16[256,1024]{1,0:T(8,128)(2,1)S(1)}, bf16[256,1024]{1,0:T(8,128)(2,1)}, u32[]{:S(2)}) copy-start(bf16[256,1024]{1,0:T(8,128)(2,1)} %param.35) | copy-start | bytes 1572868
  246.6 92.9 %all-gather.20.cloned.1.call-start = ((), (), s32[]{:S(2)}) async-start(), calls=%async_computation.17 | async-start | bytes 2621440 | tf_op jit(solution)/shard_map/all_gather | solution.py:56
  294.6 99.3 %reduce-scatter.22.cloned.1.call-start = ((), (), s32[]{:S(2)}) async-start(), calls=%async_computation.18 | async-start | bytes 2621440 | tf_op jit(solution)/shard_map/reduce_scatter | solution.py:61
  339.6 8.0 %copy-start.21 = (bf16[1024,1024]{1,0:T(8,128)(2,1)S(1)}, bf16[1024,1024]{1,0:T(8,128)(2,1)}, u32[]{:S(2)}) copy-start(bf16[1024,1024]{1,0:T(8,128)(2,1)} %all-gather.16.cloned.1.call-done) | copy-start | bytes 6291460
  346.2 1.3 copy-start.24
  351.3 124.9 %all-gather.22.cloned.1.call-start = ((), (), s32[]{:S(2)}) async-start(), calls=%async_computation.20 | async-start | bytes 2621440 | tf_op jit(solution)/shard_map/all_gather | solution.py:56
  393.9 2.1 copy-start.7
  393.9 2.1 copy-start.17
  396.4 1.0 copy-start.5
  398.3 99.2 %reduce-scatter.36.cloned.1.call-start = ((), (), s32[]{:S(2)}) async-start(), calls=%async_computation.26 | async-start | bytes 2359296
  408.3 133.6 %reduce-scatter.26.cloned.1.call-start = ((), (), s32[]{:S(2)}) async-start(), calls=%async_computation.21 | async-start | bytes 2359296 | tf_op jit(solution)/shard_map/reduce_scatter | solution.py:66
  414.2 1.0 copy-start.14
  414.3 171.2 %reduce-scatter.28.cloned.1.call-start = ((), (), s32[]{:S(2)}) async-start(), calls=%async_computation.22 | async-start | bytes 589824
  449.6 15.1 %copy-start.3 = (bf16[1024,1024]{1,0:T(8,128)(2,1)S(1)}, bf16[1024,1024]{1,0:T(8,128)(2,1)}, u32[]{:S(2)}) copy-start(bf16[1024,1024]{1,0:T(8,128)(2,1)} %all-gather.10.cloned.1.call-done) | copy-start | bytes 6291460
  466.4 149.8 %reduce-scatter.30.cloned.1.call-start = ((), (), s32[]{:S(2)}) async-start(), calls=%async_computation.23 | async-start | bytes 589824
  470.0 183.4 %reduce-scatter.32.cloned.1.call-start = ((), (), s32[]{:S(2)}) async-start(), calls=%async_computation.24 | async-start | bytes 589824
  470.0 3.5 copy-start.13
  473.5 2.8 copy-start.1
  473.5 217.0 %reduce-scatter.34.cloned.1.call-start = ((), (), s32[]{:S(2)}) async-start(), calls=%async_computation.25 | async-start | bytes 589824
  476.2 3.8 copy-start.11
  480.0 1.0 copy-start.9
  480.0 256.2 %reduce-scatter.24.cloned.1.call-start = ((), (), s32[]{:S(2)}) async-start(), calls=%async_computation.19 | async-start | bytes 2621440 | tf_op jit(solution)/shard_map/reduce_scatter | solution.py:61
  480.0 2.3 copy-start.4
  484.5 0.7 copy-start.23
  484.5 1.2 copy-start.22
  484.6 251.6 %copy-start.6 = (f32[256,1024]{1,0:T(8,128)S(1)}, f32[256,1024]{1,0:T(8,128)}, u32[]{:S(2)}) copy-start(f32[256,1024]{1,0:T(8,128)} %copy-done.5) | copy-start | bytes 3145732
Sparse Core Ops, SparseCore 0:
  9.6 48.8 all-gather.9
  60.1 44.7 all-gather.11
  106.8 27.8 all-gather.15
  168.0 43.8 all-gather.13
  213.7 26.8 all-gather.17
  246.7 43.6 reduce-scatter.19
  294.7 44.8 all-gather.19
  351.4 42.4 reduce-scatter.21
  398.4 56.0 all-gather.21
  457.6 39.7 reduce-scatter.35
  500.8 41.0 reduce-scatter.25
  544.8 34.1 reduce-scatter.27
  582.1 34.1 reduce-scatter.29
  619.2 34.1 reduce-scatter.31
  656.3 34.0 reduce-scatter.33
  692.6 43.5 reduce-scatter.23
